TPU v7x, 32 devices: a whole 2x2x4 slice. The times are simulated.
32 devices in a mesh: seq: 32 (over z, y, x, core).
Axes of the slice: x: 2, y: 2, z: 4, core: 2. Of those that a mesh axis runs over, the one named last changes fastest.
Arguments:
- tokens: bfloat16 [4, 2048, 768], P(None, 'seq'), may hold values from -6 to 6
- doc_lengths: int32 [4, 16], replicated, may hold values from 1 to 512, 2048 in all within a row
- first_gain: float32 [768], replicated, may hold values from 0.5 to 1.5
- first_shift: float32 [768], replicated, may hold values from -1.75 to 1.75
- input_weight: bfloat16 [768, 2304], replicated, may hold values from -0.21875 to 0.21875
- input_bias: float32 [2304], replicated, may hold values from -1.75 to 1.75
- short_kernel: float32 [3, 2304], replicated, may hold values from -3.5 to 3.5
- short_bias: float32 [2304], replicated, may hold values from -1.75 to 1.75
- embed_weight: float32 [33, 64], replicated, may hold values from -2 to 2
- embed_bias: float32 [64], replicated, may hold values from -3.140625 to 3.140625
- inner_weight: float32 [64, 64], replicated, may hold values from -1.5 to 1.5
- inner_bias: float32 [64], replicated, may hold values from -3.140625 to 3.140625
- filter_weight: float32 [64, 768], replicated, may hold values from -0.03125 to 0.03125
- decay_rates: float32 [768], replicated, may hold values from 3.07 to 15.35
- filter_bias: float32 [768], replicated, may hold values from -3 to 3
- output_weight: bfloat16 [768, 768], replicated, may hold values from -0.21875 to 0.21875
- output_bias: float32 [768], replicated, may hold values from -1.75 to 1.75
- second_gain: float32 [768], replicated, may hold values from 0.5 to 1.5
- second_shift: float32 [768], replicated, may hold values from -1.75 to 1.75
- up_weight: bfloat16 [768, 3072], replicated, may hold values from -0.21875 to 0.21875
- up_bias: float32 [3072], replicated, may hold values from -1.75 to 1.75
- down_weight: bfloat16 [3072, 768], replicated, may hold values from -0.109375 to 0.109375
- down_bias: float32 [768], replicated, may hold values from -1.75 to 1.75
- cotangent: bfloat16 [4, 2048, 768], P(None, 'seq'), may hold values from -6 to 6
Outputs:
- output: bfloat16 [4, 2048, 768], P(None, 'seq')
- grad_tokens: bfloat16 [4, 2048, 768], P(None, 'seq')
- grad_first_gain: float32 [768], replicated
- grad_first_shift: float32 [768], replicated
- grad_input_weight: float32 [768, 2304], replicated
- grad_input_bias: float32 [2304], replicated
- grad_short_kernel: float32 [3, 2304], replicated
- grad_short_bias: float32 [2304], replicated
- grad_embed_weight: float32 [33, 64], replicated
- grad_embed_bias: float32 [64], replicated
- grad_inner_weight: float32 [64, 64], replicated
- grad_inner_bias: float32 [64], replicated
- grad_filter_weight: float32 [64, 768], replicated
- grad_decay_rates: float32 [768], replicated
- grad_filter_bias: float32 [768], replicated
- grad_output_weight: float32 [768, 768], replicated
- grad_output_bias: float32 [768], replicated
- grad_second_gain: float32 [768], replicated
- grad_second_shift: float32 [768], replicated
- grad_up_weight: float32 [768, 3072], replicated
- grad_up_bias: float32 [3072], replicated
- grad_down_weight: float32 [3072, 768], replicated
- grad_down_bias: float32 [768], replicated
Inputs may be any that keep to these rules, and one draw needn't show every extreme that they name: `doc_lengths`: the lengths of one sequence add up to 2048, and the longest document of each sequence has exactly 512 positions.
All inputs are finite; a program needn't handle non-finite values.
Results may differ from a plain program's by a relative error of at most 0.014.
Values may be sent and summed in bfloat16 or wider, within the bound.
A program may use at most 192 MiB of HBM per device.

v0:
```python
import functools
import math
import jax
import jax.numpy as jnp
from jax import lax
from jax.sharding import PartitionSpec as P

HIGHEST_PRECISION = lax.Precision.HIGHEST
EPSILON = 1e-05


def from_behind(block, axis, distance):
    devices = range(lax.axis_size(axis))
    route = [(i - distance, i) for i in devices if i - distance in devices]
    return lax.ppermute(block, axis, route)


def shortened(x):
    return jax.tree.map(lambda a: a.astype(jnp.bfloat16) if a.dtype == jnp.float32 else a, x)


def layer_norm(values, norm_gain, norm_shift):
    center = values - jnp.mean(values, axis=-1, keepdims=True)
    spread = jnp.mean(center * center, axis=-1, keepdims=True)
    return center * lax.rsqrt(spread + EPSILON) * norm_gain + norm_shift


def embed_positions(positions, length, embed_width):
    band_count = (embed_width - 1) // 2
    harmonic = jnp.arange(1, band_count + 1, dtype=jnp.int32)
    phases = positions[:, None] * harmonic[None, :] % length
    angles = 2.0 * math.pi / length * phases.astype(jnp.float32)
    scaled = positions.astype(jnp.float32)[:, None] / length
    return jnp.concatenate([scaled, jnp.cos(angles), jnp.sin(angles)], axis=1)


def build_filter(
    embed_weight,
    embed_bias,
    inner_weight,
    inner_bias,
    filter_weight,
    decay_rates,
    embedded=None,
    scaled_positions=None,
):
    first_hidden = jnp.sin(
        jnp.dot(embedded, embed_weight, precision=HIGHEST_PRECISION) + embed_bias
    )
    second_hidden = jnp.sin(
        jnp.dot(first_hidden, inner_weight, precision=HIGHEST_PRECISION) + inner_bias
    )
    raw_filter = jnp.dot(second_hidden, filter_weight, precision=HIGHEST_PRECISION)
    return raw_filter * jnp.exp(-decay_rates[None, :] * scaled_positions[:, None])


def dft_tables(half_count, column_count):
    full_count = 2 * half_count
    total_count = full_count * column_count
    first_rows = jnp.arange(half_count, dtype=jnp.int32)
    first_freqs = jnp.arange(full_count, dtype=jnp.int32)
    second_index = jnp.arange(column_count, dtype=jnp.int32)
    first_angles = (
        2.0
        * math.pi
        / full_count
        * (first_rows[:, None] * first_freqs[None, :] % full_count).astype(jnp.float32)
    )
    second_angles = (
        2.0
        * math.pi
        / column_count
        * (second_index[:, None] * second_index[None, :] % column_count).astype(jnp.float32)
    )
    twist_angles = (
        2.0
        * math.pi
        / total_count
        * (first_freqs[:, None] * second_index[None, :] % total_count).astype(jnp.float32)
    )
    return (
        jnp.cos(first_angles),
        jnp.sin(first_angles),
        jnp.cos(second_angles),
        jnp.sin(second_angles),
        jnp.cos(twist_angles)[:, :, None],
        jnp.sin(twist_angles)[:, :, None],
    )


def first_section(values, matrix):
    return jnp.einsum("...nbc,nk->...kbc", values, matrix, precision=HIGHEST_PRECISION)


def first_back(values, matrix):
    return jnp.einsum("...kbc,nk->...nbc", values, matrix, precision=HIGHEST_PRECISION)


def second_section(values, matrix):
    return jnp.einsum("...kbc,bj->...kjc", values, matrix, precision=HIGHEST_PRECISION)


def second_back(values, matrix):
    return jnp.einsum("...kjc,bj->...kbc", values, matrix, precision=HIGHEST_PRECISION)


def forward_spectrum(values, tables):
    first_cos, first_sin, second_cos, second_sin, twist_cos, twist_sin = tables
    half_count = first_cos.shape[0]
    column_count = second_cos.shape[0]
    shaped = values.reshape(values.shape[:-2] + (half_count, column_count, values.shape[-1]))
    real_one = first_section(shaped, first_cos)
    imag_one = -first_section(shaped, first_sin)
    real_two = real_one * twist_cos + imag_one * twist_sin
    imag_two = imag_one * twist_cos - real_one * twist_sin
    real_out = second_section(real_two, second_cos) + second_section(imag_two, second_sin)
    imag_out = second_section(imag_two, second_cos) - second_section(real_two, second_sin)
    return (real_out, imag_out)


def inverse_half(real_in, imag_in, tables):
    first_cos, first_sin, second_cos, second_sin, twist_cos, twist_sin = tables
    half_count = first_cos.shape[0]
    column_count = second_cos.shape[0]
    real_one = second_back(real_in, second_cos) - second_back(imag_in, second_sin)
    imag_one = second_back(imag_in, second_cos) + second_back(real_in, second_sin)
    real_two = real_one * twist_cos - imag_one * twist_sin
    imag_two = imag_one * twist_cos + real_one * twist_sin
    result = first_back(real_two, first_cos) - first_back(imag_two, first_sin)
    result = result * (1.0 / (2 * half_count * column_count))
    return result.reshape(result.shape[:-3] + (half_count * column_count, result.shape[-1]))


def shards(
    tokens,
    doc_lengths,
    first_gain,
    first_shift,
    input_weight,
    input_bias,
    short_kernel,
    short_bias,
    embed_weight,
    embed_bias,
    inner_weight,
    inner_bias,
    filter_weight,
    decay_rates,
    filter_bias,
    output_weight,
    output_bias,
    second_gain,
    second_shift,
    up_weight,
    up_bias,
    down_weight,
    down_bias,
    cotangent,
):
    row_count, local_count, model_width = tokens.shape
    stream_width = 3 * model_width
    device_count = lax.axis_size("seq")
    seq_length = local_count * device_count
    offset = lax.axis_index("seq") * local_count
    positions = offset + jnp.arange(local_count, dtype=jnp.int32)
    doc_ends = jnp.cumsum(doc_lengths, axis=1)[:, :-1]
    starting = jnp.any(positions[None, :, None] == doc_ends[:, None, :], axis=-1) | (
        positions[None, :] == 0
    )
    keep_one = jnp.where(starting, 0.0, 1.0).astype(jnp.float32)
    keep_two = keep_one * jnp.concatenate(
        [jnp.ones((row_count, 1), jnp.float32), keep_one[:, :-1]], axis=1
    )
    keep_one_col = keep_one[:, :, None]
    keep_two_col = keep_two[:, :, None]
    token_values = tokens.astype(jnp.float32)
    first_norm, first_pullback = jax.vjp(layer_norm, token_values, first_gain, first_shift)
    normed = first_norm.astype(jnp.bfloat16)
    projected = (
        jnp.einsum("rsd,de->rse", normed, input_weight, preferred_element_type=jnp.float32)
        + input_bias
    ).astype(jnp.bfloat16)
    rim_rows = jnp.concatenate(
        [projected[:, -2:-1] * keep_one_col[:, -1:].astype(jnp.bfloat16), projected[:, -1:]], axis=1
    )
    previous = from_behind(rim_rows, "seq", 1)
    extended = jnp.concatenate([previous, projected], axis=1).astype(jnp.float32)
    lag_one = extended[:, 1:-1]
    lag_two = extended[:, :-2]
    proj_values = extended[:, 2:]
    short_out = (
        short_kernel[0] * proj_values
        + short_kernel[1] * keep_one_col * lag_one
        + short_kernel[2] * keep_two_col * lag_two
        + short_bias
    )
    gate_zero = short_out[..., :model_width]
    gate_one = short_out[..., model_width : 2 * model_width]
    value_part = short_out[..., 2 * model_width :]
    gated = value_part * gate_one
    tables = dft_tables(local_count, device_count)
    embedded = embed_positions(positions, seq_length, embed_weight.shape[0])
    scaled_positions = positions.astype(jnp.float32) / seq_length
    filter_fn = functools.partial(
        build_filter, embedded=embedded, scaled_positions=scaled_positions
    )
    filter_rows, filter_pullback = jax.vjp(
        filter_fn, embed_weight, embed_bias, inner_weight, inner_bias, filter_weight, decay_rates
    )
    spread_gated, spread_filter = (
        lax.all_to_all(
            gated.astype(jnp.bfloat16), "seq", split_axis=2, concat_axis=1, tiled=True
        ).astype(gated.dtype),
        lax.all_to_all(
            filter_rows[None].astype(jnp.bfloat16), "seq", split_axis=2, concat_axis=1, tiled=True
        ).astype(jnp.float32),
    )
    spread_filter = spread_filter[0]
    gated_real, gated_imag = forward_spectrum(spread_gated, tables)
    filter_real, filter_imag = forward_spectrum(spread_filter[None], tables)
    conv_real = gated_real * filter_real - gated_imag * filter_imag
    conv_imag = gated_real * filter_imag + gated_imag * filter_real
    conv_columns = inverse_half(conv_real, conv_imag, tables)
    conv_rows = lax.all_to_all(
        shortened(conv_columns), "seq", split_axis=1, concat_axis=2, tiled=True
    ).astype(conv_columns.dtype)
    conv_full = conv_rows + filter_bias * gated
    mixed_low = (conv_full * gate_zero).astype(jnp.bfloat16)
    branch = (
        jnp.einsum("rsd,de->rse", mixed_low, output_weight, preferred_element_type=jnp.float32)
        + output_bias
    )
    residual = token_values + branch
    second_norm, second_pullback = jax.vjp(layer_norm, residual, second_gain, second_shift)
    normed_two = second_norm.astype(jnp.bfloat16)
    pre_active = (
        jnp.einsum("rsd,df->rsf", normed_two, up_weight, preferred_element_type=jnp.float32)
        + up_bias
    )
    activated, gelu_pullback = jax.vjp(functools.partial(jax.nn.gelu, approximate=True), pre_active)
    hidden = activated.astype(jnp.bfloat16)
    output = (
        residual
        + jnp.einsum("rsf,fd->rsd", hidden, down_weight, preferred_element_type=jnp.float32)
        + down_bias
    ).astype(jnp.bfloat16)
    cot_values = cotangent.astype(jnp.float32)
    grad_down_weight = jnp.einsum(
        "rsf,rsd->fd", hidden, cotangent, preferred_element_type=jnp.float32
    )
    grad_down_bias = jnp.sum(cot_values, axis=(0, 1))
    grad_hidden = jnp.einsum(
        "rsd,fd->rsf", cotangent, down_weight, preferred_element_type=jnp.float32
    )
    grad_pre = gelu_pullback(grad_hidden)[0].astype(jnp.bfloat16)
    grad_up_weight = jnp.einsum(
        "rsd,rsf->df", normed_two, grad_pre, preferred_element_type=jnp.float32
    )
    grad_up_bias = jnp.sum(grad_pre.astype(jnp.float32), axis=(0, 1))
    grad_normed_two = jnp.einsum(
        "rsf,df->rsd", grad_pre, up_weight, preferred_element_type=jnp.float32
    )
    grad_residual_part, grad_second_gain, grad_second_shift = second_pullback(grad_normed_two)
    grad_residual = cot_values + grad_residual_part
    grad_branch = grad_residual.astype(jnp.bfloat16)
    grad_output_weight = jnp.einsum(
        "rsd,rse->de", mixed_low, grad_branch, preferred_element_type=jnp.float32
    )
    grad_output_bias = jnp.sum(grad_branch.astype(jnp.float32), axis=(0, 1))
    grad_mixed = jnp.einsum(
        "rse,de->rsd", grad_branch, output_weight, preferred_element_type=jnp.float32
    )
    grad_conv = grad_mixed * gate_zero
    grad_gate_zero = grad_mixed * conv_full
    grad_filter_bias = jnp.sum(grad_conv * gated, axis=(0, 1))
    grad_conv_columns = lax.all_to_all(
        grad_conv.astype(jnp.bfloat16), "seq", split_axis=2, concat_axis=1, tiled=True
    ).astype(grad_conv.dtype)
    grad_real, grad_imag = forward_spectrum(grad_conv_columns, tables)
    back_real = filter_real * grad_real + filter_imag * grad_imag
    back_imag = filter_real * grad_imag - filter_imag * grad_real
    grad_gated_columns = inverse_half(back_real, back_imag, tables)
    taps_real = jnp.sum(gated_real * grad_real + gated_imag * grad_imag, axis=0, keepdims=True)
    taps_imag = jnp.sum(gated_real * grad_imag - gated_imag * grad_real, axis=0, keepdims=True)
    grad_filter_columns = inverse_half(taps_real, taps_imag, tables)
    grad_gated_rows, grad_filter_rows = (
        lax.all_to_all(
            shortened(grad_gated_columns), "seq", split_axis=1, concat_axis=2, tiled=True
        ).astype(grad_gated_columns.dtype),
        lax.all_to_all(
            shortened(grad_filter_columns), "seq", split_axis=1, concat_axis=2, tiled=True
        ).astype(grad_filter_columns.dtype),
    )
    filter_grads = filter_pullback(grad_filter_rows[0])
    grad_filter_weight = filter_grads[4]
    grad_decay_rates = filter_grads[5]
    grad_gated = grad_gated_rows + filter_bias * grad_conv
    grad_short = jnp.concatenate(
        [grad_gate_zero, grad_gated * value_part, grad_gated * gate_one], axis=-1
    )
    grad_short_bias = jnp.sum(grad_short, axis=(0, 1))
    grad_short_kernel = jnp.stack(
        [
            jnp.sum(grad_short * proj_values, axis=(0, 1)),
            jnp.sum(grad_short * keep_one_col * lag_one, axis=(0, 1)),
            jnp.sum(grad_short * keep_two_col * lag_two, axis=(0, 1)),
        ]
    )
    tap_one = short_kernel[1] * keep_one_col * grad_short
    tap_two = short_kernel[2] * keep_two_col * grad_short
    outgoing = jnp.concatenate([tap_two[:, 0:1], tap_one[:, 0:1] + tap_two[:, 1:2]], axis=1)
    incoming = from_behind(shortened(outgoing), "seq", -1).astype(outgoing.dtype)
    grad_proj = (
        short_kernel[0] * grad_short
        + jnp.concatenate(
            [tap_one[:, 1:], jnp.zeros((row_count, 1, stream_width), jnp.float32)], axis=1
        )
        + jnp.concatenate(
            [tap_two[:, 2:], jnp.zeros((row_count, 2, stream_width), jnp.float32)], axis=1
        )
    )
    rim_terms = jnp.concatenate(
        [
            jnp.zeros((row_count, local_count - 2, stream_width), jnp.float32),
            incoming[:, 0:1] * keep_one_col[:, -1:],
            incoming[:, 1:2],
        ],
        axis=1,
    )
    grad_proj_low = (grad_proj + rim_terms).astype(jnp.bfloat16)
    grad_input_weight = jnp.einsum(
        "rsd,rse->de", normed, grad_proj_low, preferred_element_type=jnp.float32
    )
    grad_input_bias = jnp.sum(grad_proj_low.astype(jnp.float32), axis=(0, 1))
    grad_normed = jnp.einsum(
        "rse,de->rsd", grad_proj_low, input_weight, preferred_element_type=jnp.float32
    )
    grad_token_part, grad_first_gain, grad_first_shift = first_pullback(grad_normed)
    grad_tokens = (grad_residual + grad_token_part).astype(jnp.bfloat16)
    summed = lax.psum(
        (
            grad_first_gain,
            grad_first_shift,
            grad_input_weight,
            grad_input_bias,
            grad_short_kernel,
            grad_short_bias,
            filter_grads[0],
            filter_grads[1],
            filter_grads[2],
            filter_grads[3],
            grad_filter_weight,
            grad_decay_rates,
            grad_filter_bias,
            grad_output_weight,
            grad_output_bias,
            grad_second_gain,
            grad_second_shift,
            grad_up_weight,
            grad_up_bias,
            grad_down_weight,
            grad_down_bias,
        ),
        "seq",
    )
    summed = tuple(summed)
    return (output, grad_tokens) + summed


def solution(mesh):
    return jax.shard_map(
        shards,
        mesh=mesh,
        in_specs=(
            P(None, "seq", None),
            P(),
            P(),
            P(),
            P(),
            P(),
            P(),
            P(),
            P(),
            P(),
            P(),
            P(),
            P(),
            P(),
            P(),
            P(),
            P(),
            P(),
            P(),
            P(),
            P(),
            P(),
            P(),
            P(None, "seq", None),
        ),
        out_specs=(
            P(None, "seq", None),
            P(None, "seq", None),
            P(),
            P(),
            P(),
            P(),
            P(),
            P(),
            P(),
            P(),
            P(),
            P(),
            P(),
            P(),
            P(),
            P(),
            P(),
            P(),
            P(),
            P(),
            P(),
            P(),
            P(),
        ),
        check_vma=False,
    )
```

profile of v0, /device:TPU:0, one launch (start us, length us, event | category | flops | bytes accessed | tf_op | source)
XLA Modules:
  0.0 992.1 jit_solution(14004255950969521183)
XLA Ops:
  17.2 3.4 reduce.10
  22.4 7.4 all-to-all-start.1
  47.1 2.9 reshape.372
  50.0 8.3 all-to-all-start
  71.5 3.0 reshape.373
  76.7 3.4 reshape.327
  80.1 3.0 convolution_negate_fusion.1
  101.9 5.5 copy.287
  107.3 6.6 reshape.376
  113.9 5.7 all-to-all-start.2
  121.5 11.3 %all-to-all-done.2 = bf16[32,2,3072]{2,1,0:T(2,128)(2,1)} async-done(((bf16[32,2,3072]{2,1,0:T(2,128)(2,1)}), bf16[32,2,3072]{2,1,0:T(2,128)(2,1)}, u32[]{:S(2)}, u32[]{:S(2)}) %all-to-all-start.2) | async-done | bytes 393248 | tf_op jit(solution)/shard_map/all_to_all | solution.py:224
  132.8 7.7 reshape.377
  140.5 3.9 copy.234
  144.4 2.9 reshape.335
  147.3 3.5 copy.235
  156.5 4.0 fusion.8
  160.5 7.0 convert_reduce_fusion
  169.7 5.3 convolution_bitcast_fusion.1
  177.1 3.4 multiply_reduce_fusion.4
  184.3 2.9 reshape.378
  187.2 3.7 all-to-all-start.3
  190.9 3.2 convolution_bitcast_fusion.3
  194.1 7.0 convolution_bitcast_fusion
  201.1 3.0 all-to-all-done.3
  204.1 3.0 reshape.379
  209.4 3.2 reshape.329
  212.6 2.9 convolution_negate_fusion
  227.2 2.9 fusion.156
  236.8 4.1 reshape.366
  240.9 13.4 %reduce.11 = bf16[2048,24]{1,0:T(8,128)(2,1)} reduce(bf16[2048,1,24]{2,1,0:T(2,128)(2,1)} %bitcast.425, bf16[]{:T(256)} %broadcast.460), dimensions={1}, to_apply=%bitcast.363.reduce_sub_computation | reduce | bytes 196610
  256.7 3.5 all-to-all-start.5
  260.2 4.4 convolution_add_fusion.1
  270.4 5.5 copy.292
  275.8 6.6 reshape.380
  282.4 6.1 all-to-all-start.4
  288.6 4.0 reshape.383
  292.6 3.3 copy.253
  312.0 7.7 reshape.381
  319.7 3.9 copy.248
  323.6 2.8 reshape.336
  326.3 3.5 copy.249
  347.4 5.6 convolution_bitcast_fusion.2
  353.8 6.1 fusion.93
  359.9 143.6 %all-reduce.8.cloned.1.call-done = (f32[768]{0:T(1024)}, f32[768]{0:T(1024)}, f32[2304]{0:T(1024)}, f32[3,2304]{1,0:T(4,128)}, f32[2304]{0:T(1024)}, /*index=5*/...) async-done(((f32[768]{0:T(1024)}, f32[768]{0:T(1024)}, ...) | async-done | bytes 108304 | tf_op jit(solution)/shard_map/psum | solution.py:340
  503.5 449.5 %all-reduce.10.cloned.1.call-done = (f32[768,2304]{1,0:T(8,128)}, f32[64,768]{1,0:T(8,128)}, f32[768,768]{1,0:T(8,128)}, f32[768,3072]{1,0:T(8,128)}, f32[3072,768]{1,0:T(8,128)}) async-done(((f32[768,2304]{1,0:T(8,128)}, f32[64,768]{1,0:T(8,128)}, f32[768,768]{1,0:T(8,128)}, f32[768,3072]{1,0:T(8,128)}, f32[3072,768]{1,0:T(8,128)}), (f32[768,2304]{1,0:T(8,128)}, f32[64,768]{1,0:T(8,128)}, ...) | async-done | bytes 28508176 | tf_op jit(solution)/shard_map/psum | solution.py:340
  955.6 6.6 copy.321
  971.4 8.8 copy.336
  980.8 3.7 copy.338
  (373 shorter events, 153.8 us)
Async XLA Ops:
  7.2 28.7 %copy-start = (bf16[768,2304]{1,0:T(8,128)(2,1)S(1)}, bf16[768,2304]{1,0:T(8,128)(2,1)}, u32[]{:S(2)}) copy-start(bf16[768,2304]{1,0:T(8,128)(2,1)} %param.28) | copy-start | bytes 10616836
  7.2 6.2 copy-start.84
  8.1 5.3 copy-start.55
  11.6 21.1 %copy-start.98 = (s32[4,16]{1,0:T(4,128)S(1)}, s32[4,16]{1,0:T(4,128)}, u32[]{:S(2)}) copy-start(s32[4,16]{1,0:T(4,128)} %param.25) | copy-start | bytes 772
  22.4 27.6 %all-to-all-start.1 = ((bf16[32,2,768]{2,1,0:T(2,128)(2,1)}), bf16[32,2,768]{2,1,0:T(2,128)(2,1)}, u32[]{:S(2)}, u32[]{:S(2)}) async-start(bf16[32,2,768]{2,1,0:T(2,128)(2,1)} %reshape.374), calls=%async_computation.1 | async-start | bytes 196608 | tf_op jit(solution)/shard_map/all_to_all | solution.py:214
  31.5 6.7 copy-start.63
  32.7 5.4 copy-start.70
  35.9 4.6 copy-start.87
  35.9 4.7 copy-start.68
  38.3 3.0 collective-permute-start
  50.0 21.5 %all-to-all-start = ((bf16[32,2,3072]{2,1,0:T(2,128)(2,1)}), bf16[32,2,3072]{2,1,0:T(2,128)(2,1)}, u32[]{:S(2)}, u32[]{:S(2)}) async-start(bf16[32,2,3072]{2,1,0:T(2,128)(2,1)} %reshape.372), calls=%async_computation | async-start | bytes 786432 | tf_op jit(solution)/shard_map/all_to_all | solution.py:211
  89.3 7.0 copy-start.3
  91.0 5.3 copy-start.5
  113.9 18.8 %all-to-all-start.2 = ((bf16[32,2,3072]{2,1,0:T(2,128)(2,1)}), bf16[32,2,3072]{2,1,0:T(2,128)(2,1)}, u32[]{:S(2)}, u32[]{:S(2)}) async-start(bf16[32,2,3072]{2,1,0:T(2,128)(2,1)} %reshape.376), calls=%async_computation.2 | async-start | bytes 786432 | tf_op jit(solution)/shard_map/all_to_all | solution.py:224
  156.2 18.8 %copy-start.20 = (f32[4,64,768]{2,1,0:T(8,128)}, f32[4,64,768]{2,1,0:T(8,128)S(1)}, u32[]{:S(2)}) copy-start(f32[4,64,768]{2,1,0:T(8,128)S(1)} %get-tuple-element.86) | copy-start | bytes 2359300
  156.5 11.0 %slice-start.3 = ((s8[4718592]{0:T(1024)(128)(4,1)}), s8[4194304]{0:T(1024)(128)(4,1)S(1)}, s32[]{:S(2)}) async-start(s8[4718592]{0:T(1024)(128)(4,1)} %bitcast.423), calls=%async_computation.11 | async-start | bytes 8388608
  160.5 7.0 copy-start.35
  160.5 7.0 slice-start.4
  175.5 5.0 copy-start.74
  187.2 16.9 %all-to-all-start.3 = ((bf16[32,2,3072]{2,1,0:T(2,128)(2,1)}), bf16[32,2,3072]{2,1,0:T(2,128)(2,1)}, u32[]{:S(2)}, u32[]{:S(2)}) async-start(bf16[32,2,3072]{2,1,0:T(2,128)(2,1)} %reshape.378), calls=%async_computation.3 | async-start | bytes 786432 | tf_op jit(solution)/shard_map/all_to_all | solution.py:276
  222.0 5.1 copy-start.7
  256.7 25.7 %all-to-all-start.5 = ((bf16[32,2,768]{2,1,0:T(2,128)(2,1)}), bf16[32,2,768]{2,1,0:T(2,128)(2,1)}, u32[]{:S(2)}, u32[]{:S(2)}) async-start(bf16[32,2,768]{2,1,0:T(2,128)(2,1)} %reshape.382), calls=%async_computation.5 | async-start | bytes 196608 | tf_op jit(solution)/shard_map/all_to_all | solution.py:290
  260.2 4.5 copy-start.8
  260.2 4.5 copy-start.10
  260.2 4.5 copy-start.13
  260.2 4.5 copy-start.16
  282.4 29.5 %all-to-all-start.4 = ((bf16[32,2,3072]{2,1,0:T(2,128)(2,1)}), bf16[32,2,3072]{2,1,0:T(2,128)(2,1)}, u32[]{:S(2)}, u32[]{:S(2)}) async-start(bf16[32,2,3072]{2,1,0:T(2,128)(2,1)} %reshape.380), calls=%async_computation.4 | async-start | bytes 786432 | tf_op jit(solution)/shard_map/all_to_all | solution.py:287
  288.5 215.0 %all-reduce.8.cloned.1.call-start = ((), (), s32[]{:S(2)}) async-start(), calls=%async_computation.6 | async-start | bytes 321536 | tf_op jit(solution)/shard_map/psum | solution.py:340
  292.5 9.0 copy-start.56
  292.6 9.0 copy-start.85
  295.9 10.9 %copy-start.58 = (f32[64,16]{0,1:T(8,128)S(1)}, f32[64,16]{0,1:T(8,128)}, u32[]{:S(2)}) copy-start(f32[64,16]{0,1:T(8,128)} %copy-done.57) | copy-start | bytes 12292
  337.9 3.1 collective-permute-start.1
  347.2 605.8 %all-reduce.10.cloned.1.call-start = ((), (), s32[]{:S(2)}) async-start(), calls=%async_computation.7 | async-start | bytes 57016320 | tf_op jit(solution)/shard_map/psum | solution.py:340
  955.5 6.7 copy-start.83
  955.5 7.3 copy-start.60
  955.5 7.9 copy-start.82
  955.5 8.5 copy-start.69
  955.5 9.1 copy-start.103
  955.6 9.6 copy-start.67
  955.6 10.2 %copy-start.102 = (f32[64]{0:T(128)S(1)}, f32[64]{0:T(128)}, u32[]{:S(2)}) copy-start(f32[64]{0:T(128)} %get-tuple-element.109) | copy-start | bytes 772
  955.6 10.7 %copy-start.47 = (f32[64,768]{1,0:T(8,128)S(1)}, f32[64,768]{1,0:T(8,128)}, u32[]{:S(2)}) copy-start(f32[64,768]{1,0:T(8,128)} %get-tuple-element.110) | copy-start | bytes 589828
  955.6 11.4 %copy-start.94 = (f32[768]{0:T(1024)S(1)}, f32[768]{0:T(1024)}, u32[]{:S(2)}) copy-start(f32[768]{0:T(1024)} %get-tuple-element.111) | copy-start | bytes 9220
  955.6 12.0 %copy-start.93 = (f32[768]{0:T(1024)S(1)}, f32[768]{0:T(1024)}, u32[]{:S(2)}) copy-start(f32[768]{0:T(1024)} %get-tuple-element.112) | copy-start | bytes 9220
  955.6 12.5 %copy-start.37 = (f32[768,768]{1,0:T(8,128)S(1)}, f32[768,768]{1,0:T(8,128)}, u32[]{:S(2)}) copy-start(f32[768,768]{1,0:T(8,128)} %get-tuple-element.113) | copy-start | bytes 7077892
  968.2 12.6 %slice-start = ((s8[9437184]{0:T(1024)(128)(4,1)}), s8[4194304]{0:T(1024)(128)(4,1)S(1)}, s32[]{:S(2)}) async-start(s8[9437184]{0:T(1024)(128)(4,1)} %bitcast.413), calls=%async_computation.8 | async-start | bytes 8388608
  971.4 8.8 copy-start.81
  971.4 9.4 slice-start.1
  971.4 9.4 slice-start.2
  (71 other events, 139.6 us)
Sparse Core Ops, SparseCore 0:
  347.3 156.1 all-reduce.7
  513.1 439.8 all-reduce.9
where the time goes:
time: 1000 us; the launch traced here: 992 us
  waiting for transfers between devices  609 us (61%)
  local copies, waits for them, and re-layouts  166 us (17%)
  matrix products  121 us (12%)
  other arithmetic  42.1 us (4%)
  starting transfers between devices  38.3 us (4%)
  between operations  15.8 us (2%)
    psum x2, waiting for transfers between devices, shards(): lax.psum((grad_first_gain, grad_first_shift, grad_input_weight, grad_inpu...  593 us
    unnamed x253, local copies, waits for them, and re-layouts  90.6 us
    dot_general x12, matrix products, second_back(): jnp.einsum('...kjc,bj->...kbc', values, matrix, precision=HIGHEST_PRECISION)  20.8 us
  transfers between devices with their start and end apart: 10, of which 6 were waited for; matrix products, arithmetic and copies ran while one was open for 10% of the time, Pallas kernels for 0%

commit v1 on v0

--- a/solution.py
+++ b/solution.py
@@ -221,8 +221,11 @@
     conv_real = gated_real * filter_real - gated_imag * filter_imag
     conv_imag = gated_real * filter_imag + gated_imag * filter_real
     conv_columns = inverse_half(conv_real, conv_imag, tables)
-    conv_rows = lax.all_to_all(
-        shortened(conv_columns), "seq", split_axis=1, concat_axis=2, tiled=True
+    conv_rows = jnp.concatenate(
+        lax.all_to_all(
+            jnp.stack(jnp.split(shortened(conv_columns), lax.axis_size("seq"), axis=1)), "seq", 0, 0
+        ),
+        axis=2,
     ).astype(conv_columns.dtype)
     conv_full = conv_rows + filter_bias * gated
     mixed_low = (conv_full * gate_zero).astype(jnp.bfloat16)

time: 1000 us -> 1030 us (1.030)
  local copies, waits for them, and re-layouts: 166 us -> 194 us
    unnamed x253 -> x284, local copies, waits for them, and re-layouts: 90.6 us -> 125 us
where the time goes in v1:
time: 1030 us; the launch traced here: 1020 us
  waiting for transfers between devices  609 us (59%)
  local copies, waits for them, and re-layouts  194 us (19%)
  matrix products  121 us (12%)
  other arithmetic  43.5 us (4%)
  starting transfers between devices  38.4 us (4%)
  between operations  15.8 us (2%)
    psum x2, waiting for transfers between devices, shards(): lax.psum((grad_first_gain, grad_first_shift, grad_input_weight, grad_inpu...  593 us
    unnamed x284, local copies, waits for them, and re-layouts  125 us
    dot_general x12, matrix products, second_back(): jnp.einsum('...kjc,bj->...kbc', values, matrix, precision=HIGHEST_PRECISION)  20.7 us
  transfers between devices with their start and end apart: 10, of which 6 were waited for; matrix products, arithmetic and copies ran while one was open for 10% of the time, Pallas kernels for 0%

profile of v1, /device:TPU:0, one launch (start us, length us, event | category | flops | bytes accessed | tf_op | source)
XLA Modules:
  0.0 1020.9 jit_solution(8745569360675244281)
XLA Ops:
  17.2 3.4 reduce.10
  22.4 7.4 all-to-all-start.1
  47.1 2.9 reshape.371
  50.0 8.7 all-to-all-start
  71.8 3.0 reshape.372
  77.1 3.3 reshape.327
  80.5 3.0 convolution_negate_fusion.1
  104.6 3.6 convert_element_type.299
  152.6 2.7 reshape.375
  155.2 5.8 all-to-all-start.2
  163.0 11.3 %all-to-all-done.2 = bf16[32,2,3072]{2,1,0:T(2,128)(2,1)} async-done(((bf16[32,2,3072]{2,1,0:T(2,128)(2,1)}), bf16[32,2,3072]{2,1,0:T(2,128)(2,1)}, u32[]{:S(2)}, u32[]{:S(2)}) %all-to-all-start.2) | async-done | bytes 393248 | tf_op jit(solution)/shard_map/all_to_all | solution.py:225
  174.3 2.7 reshape.376
  179.5 2.8 copy.261
  185.3 4.0 fusion.8
  189.3 7.0 convert_reduce_fusion
  198.5 5.3 convolution_bitcast_fusion.1
  205.9 3.3 multiply_reduce_fusion.4
  213.1 2.9 reshape.377
  216.0 3.3 all-to-all-start.3
  219.3 3.2 convolution_bitcast_fusion.3
  222.5 7.0 convolution_bitcast_fusion
  229.4 3.0 all-to-all-done.3
  232.5 3.0 reshape.378
  237.8 3.6 reshape.329
  241.4 2.9 convolution_negate_fusion
  253.2 2.8 fusion.152
  255.9 2.9 fusion.156
  265.6 4.1 reshape.365
  269.7 13.4 %reduce.11 = bf16[2048,24]{1,0:T(8,128)(2,1)} reduce(bf16[2048,1,24]{2,1,0:T(2,128)(2,1)} %bitcast.553, bf16[]{:T(256)} %broadcast.460), dimensions={1}, to_apply=%bitcast.493.reduce_sub_computation | reduce | bytes 196610
  285.5 3.5 all-to-all-start.5
  289.0 4.4 convolution_add_fusion.1
  299.1 5.5 copy.316
  304.6 6.6 reshape.379
  311.2 6.1 all-to-all-start.4
  317.3 4.0 reshape.382
  321.3 3.3 copy.278
  340.7 7.7 reshape.380
  348.5 3.9 copy.273
  352.3 2.8 reshape.335
  355.1 3.5 copy.274
  358.6 2.8 copy.275
  376.2 5.6 convolution_bitcast_fusion.2
  382.5 6.1 fusion.93
  388.7 143.6 %all-reduce.8.cloned.1.call-done = (f32[768]{0:T(1024)}, f32[768]{0:T(1024)}, f32[2304]{0:T(1024)}, f32[3,2304]{1,0:T(4,128)}, f32[2304]{0:T(1024)}, /*index=5*/...) async-done(((f32[768]{0:T(1024)}, f32[768]{0:T(1024)}, ...) | async-done | bytes 108304 | tf_op jit(solution)/shard_map/psum | solution.py:343
  532.3 449.5 %all-reduce.10.cloned.1.call-done = (f32[768,2304]{1,0:T(8,128)}, f32[64,768]{1,0:T(8,128)}, f32[768,768]{1,0:T(8,128)}, f32[768,3072]{1,0:T(8,128)}, f32[3072,768]{1,0:T(8,128)}) async-done(((f32[768,2304]{1,0:T(8,128)}, f32[64,768]{1,0:T(8,128)}, f32[768,768]{1,0:T(8,128)}, f32[768,3072]{1,0:T(8,128)}, f32[3072,768]{1,0:T(8,128)}), (f32[768,2304]{1,0:T(8,128)}, f32[64,768]{1,0:T(8,128)}, ...) | async-done | bytes 28508176 | tf_op jit(solution)/shard_map/psum | solution.py:343
  984.4 6.6 copy.375
  1000.2 8.8 copy.390
  1009.5 3.7 copy.392
  (405 shorter events, 194.9 us)
Async XLA Ops:
  7.2 28.7 %copy-start = (bf16[768,2304]{1,0:T(8,128)(2,1)S(1)}, bf16[768,2304]{1,0:T(8,128)(2,1)}, u32[]{:S(2)}) copy-start(bf16[768,2304]{1,0:T(8,128)(2,1)} %param.28) | copy-start | bytes 10616836
  7.2 6.2 copy-start.84
  8.1 5.3 copy-start.55
  11.6 21.1 %copy-start.98 = (s32[4,16]{1,0:T(4,128)S(1)}, s32[4,16]{1,0:T(4,128)}, u32[]{:S(2)}) copy-start(s32[4,16]{1,0:T(4,128)} %param.25) | copy-start | bytes 772
  22.4 27.6 %all-to-all-start.1 = ((bf16[32,2,768]{2,1,0:T(2,128)(2,1)}), bf16[32,2,768]{2,1,0:T(2,128)(2,1)}, u32[]{:S(2)}, u32[]{:S(2)}) async-start(bf16[32,2,768]{2,1,0:T(2,128)(2,1)} %reshape.373), calls=%async_computation.1 | async-start | bytes 196608 | tf_op jit(solution)/shard_map/all_to_all | solution.py:214
  31.5 6.7 copy-start.63
  32.7 5.4 copy-start.70
  35.9 4.6 copy-start.87
  35.9 4.7 copy-start.68
  38.3 3.0 collective-permute-start
  50.0 21.8 %all-to-all-start = ((bf16[32,2,3072]{2,1,0:T(2,128)(2,1)}), bf16[32,2,3072]{2,1,0:T(2,128)(2,1)}, u32[]{:S(2)}, u32[]{:S(2)}) async-start(bf16[32,2,3072]{2,1,0:T(2,128)(2,1)} %reshape.371), calls=%async_computation | async-start | bytes 786432 | tf_op jit(solution)/shard_map/all_to_all | solution.py:211
  89.6 6.9 copy-start.3
  91.3 5.2 copy-start.5
  155.2 19.0 %all-to-all-start.2 = ((bf16[32,2,3072]{2,1,0:T(2,128)(2,1)}), bf16[32,2,3072]{2,1,0:T(2,128)(2,1)}, u32[]{:S(2)}, u32[]{:S(2)}) async-start(bf16[32,2,3072]{2,1,0:T(2,128)(2,1)} %reshape.375), calls=%async_computation.2 | async-start | bytes 786432 | tf_op jit(solution)/shard_map/all_to_all | solution.py:225
  185.0 18.8 %copy-start.20 = (f32[4,64,768]{2,1,0:T(8,128)}, f32[4,64,768]{2,1,0:T(8,128)S(1)}, u32[]{:S(2)}) copy-start(f32[4,64,768]{2,1,0:T(8,128)S(1)} %get-tuple-element.86) | copy-start | bytes 2359300
  185.3 11.0 %slice-start.3 = ((s8[4718592]{0:T(1024)(128)(4,1)}), s8[4194304]{0:T(1024)(128)(4,1)S(1)}, s32[]{:S(2)}) async-start(s8[4718592]{0:T(1024)(128)(4,1)} %bitcast.551), calls=%async_computation.11 | async-start | bytes 8388608
  189.3 7.0 copy-start.35
  189.3 7.0 slice-start.4
  204.3 5.0 copy-start.74
  216.0 16.5 %all-to-all-start.3 = ((bf16[32,2,3072]{2,1,0:T(2,128)(2,1)}), bf16[32,2,3072]{2,1,0:T(2,128)(2,1)}, u32[]{:S(2)}, u32[]{:S(2)}) async-start(bf16[32,2,3072]{2,1,0:T(2,128)(2,1)} %reshape.377), calls=%async_computation.3 | async-start | bytes 786432 | tf_op jit(solution)/shard_map/all_to_all | solution.py:279
  250.8 5.1 copy-start.7
  285.5 25.7 %all-to-all-start.5 = ((bf16[32,2,768]{2,1,0:T(2,128)(2,1)}), bf16[32,2,768]{2,1,0:T(2,128)(2,1)}, u32[]{:S(2)}, u32[]{:S(2)}) async-start(bf16[32,2,768]{2,1,0:T(2,128)(2,1)} %reshape.381), calls=%async_computation.5 | async-start | bytes 196608 | tf_op jit(solution)/shard_map/all_to_all | solution.py:293
  289.0 4.5 copy-start.8
  289.0 4.5 copy-start.10
  289.0 4.5 copy-start.13
  289.0 4.5 copy-start.16
  311.2 29.5 %all-to-all-start.4 = ((bf16[32,2,3072]{2,1,0:T(2,128)(2,1)}), bf16[32,2,3072]{2,1,0:T(2,128)(2,1)}, u32[]{:S(2)}, u32[]{:S(2)}) async-start(bf16[32,2,3072]{2,1,0:T(2,128)(2,1)} %reshape.379), calls=%async_computation.4 | async-start | bytes 786432 | tf_op jit(solution)/shard_map/all_to_all | solution.py:290
  317.3 215.0 %all-reduce.8.cloned.1.call-start = ((), (), s32[]{:S(2)}) async-start(), calls=%async_computation.6 | async-start | bytes 321536 | tf_op jit(solution)/shard_map/psum | solution.py:343
  321.3 9.0 copy-start.56
  321.3 9.0 copy-start.85
  324.7 10.9 %copy-start.58 = (f32[64,16]{0,1:T(8,128)S(1)}, f32[64,16]{0,1:T(8,128)}, u32[]{:S(2)}) copy-start(f32[64,16]{0,1:T(8,128)} %copy-done.57) | copy-start | bytes 12292
  366.7 3.1 collective-permute-start.1
  376.0 605.8 %all-reduce.10.cloned.1.call-start = ((), (), s32[]{:S(2)}) async-start(), calls=%async_computation.7 | async-start | bytes 57016320 | tf_op jit(solution)/shard_map/psum | solution.py:343
  984.3 6.7 copy-start.83
  984.3 7.3 copy-start.60
  984.3 7.9 copy-start.82
  984.3 8.5 copy-start.69
  984.3 9.1 copy-start.103
  984.3 9.6 copy-start.67
  984.4 10.2 copy-start.102
  984.4 10.7 %copy-start.47 = (f32[64,768]{1,0:T(8,128)S(1)}, f32[64,768]{1,0:T(8,128)}, u32[]{:S(2)}) copy-start(f32[64,768]{1,0:T(8,128)} %get-tuple-element.110) | copy-start | bytes 589828
  984.4 11.4 %copy-start.94 = (f32[768]{0:T(1024)S(1)}, f32[768]{0:T(1024)}, u32[]{:S(2)}) copy-start(f32[768]{0:T(1024)} %get-tuple-element.111) | copy-start | bytes 9220
  984.4 12.0 %copy-start.93 = (f32[768]{0:T(1024)S(1)}, f32[768]{0:T(1024)}, u32[]{:S(2)}) copy-start(f32[768]{0:T(1024)} %get-tuple-element.112) | copy-start | bytes 9220
  984.4 12.5 %copy-start.37 = (f32[768,768]{1,0:T(8,128)S(1)}, f32[768,768]{1,0:T(8,128)}, u32[]{:S(2)}) copy-start(f32[768,768]{1,0:T(8,128)} %get-tuple-element.113) | copy-start | bytes 7077892
  996.9 12.6 %slice-start = ((s8[9437184]{0:T(1024)(128)(4,1)}), s8[4194304]{0:T(1024)(128)(4,1)S(1)}, s32[]{:S(2)}) async-start(s8[9437184]{0:T(1024)(128)(4,1)} %bitcast.544), calls=%async_computation.8 | async-start | bytes 8388608
  1000.2 8.8 copy-start.81
  1000.2 9.4 slice-start.1
  1000.2 9.4 slice-start.2
  (71 other events, 139.6 us)
Sparse Core Ops, SparseCore 0:
  376.1 156.1 all-reduce.7
  541.9 439.8 all-reduce.9
